TPU v7x, 32 devices: a whole 2x2x4 slice. The times are simulated.
32 devices in a mesh: row: 4 (over y, x), col: 8 (over z, core).
Axes of the slice: x: 2, y: 2, z: 4, core: 2. Of those that a mesh axis runs over, the one named last changes fastest.
Arguments:
- image: bfloat16 [256, 512, 256], P('row', 'col'), may hold values from -6 to 6
- vert_rate: float32 [8, 256], replicated, may hold values from 0.001171875 to 0.065625
- vert_coef: float32 [8, 256], replicated, may hold values from -28.8 to 28.8
- horiz_rate: float32 [8, 256], replicated, may hold values from 0.0005859375 to 0.065625
- horiz_coef: float32 [8, 256], replicated, may hold values from -28.8 to 28.8
- w_in: bfloat16 [256, 1024], replicated, may hold values from -0.375 to 0.375
- w_out: bfloat16 [1024, 256], replicated, may hold values from -0.1875 to 0.1875
Outputs:
- mixed: bfloat16 [256, 512, 256], P('row', 'col')
All inputs are finite; a program needn't handle non-finite values.
Results may differ from a plain program's by a relative error of at most 0.006.
Values sent between devices are 32-bit elements; how exact they have to be, the bound alone decides.
A program may use at most 128 MiB of HBM per device.

v0:
```python
import functools

import jax
import jax.numpy as jnp
from jax import lax
from jax.experimental import pallas as pl
from jax.experimental.pallas import tpu as pltpu
from jax.sharding import PartitionSpec as P

LANES = 128
GROUP = 16
BLOCK = 16
AHEAD = 3
PIECES = 2
MESH = pl.DeviceIdType.MESH
C0 = 0.7978845608028654
C1 = 0.7978845608028654 * 0.044715


def twice_gelu(x):
    return x + x * jnp.tanh(x * (C0 + C1 * (x * x)))


def layer_kernel(
    nrow, ncol, rows, cols, modes, halves,
    image_hbm, vrate_hbm, vcoef_hbm, hrate_hbm, hcoef_hbm, w_in_hbm, w_out_hbm, half_hbm,
    img, vrate, vcoef, hrate, hcoef, w_in, w_out, half, out,
    ptab, qtab, dtab, lead, vedge, vin, hedge, hin,
    vsend, vrecv, hsend, hrecv, img_sem, arg_sem, out_sem,
):
    row = lax.axis_index("row")
    col = lax.axis_index("col")
    nk = cols // GROUP
    nr = rows // GROUP
    pitch = cols + 1
    size = rows * pitch

    def fetch_image(k):
        part = pl.ds(pl.multiple_of(k * GROUP, GROUP), GROUP)
        return pltpu.make_async_copy(image_hbm.at[:, part, :], img.at[:, part, :], img_sem.at[k])

    fetches = [
        pltpu.make_async_copy(src, dst, arg_sem.at[i])
        for i, (src, dst) in enumerate((
            (vrate_hbm, vrate), (vcoef_hbm, vcoef), (hrate_hbm, hrate), (hcoef_hbm, hcoef),
            (w_in_hbm, w_in), (w_out_hbm, w_out),
        ))
    ]
    for copy in fetches[:4]:
        copy.start()
    for k in range(nk):
        fetch_image(k).start()
    for copy in fetches[4:]:
        copy.start()

    barrier = pltpu.get_barrier_semaphore()
    neighbours = (
        (row > 0, {"row": row - 1}),
        (row < nrow - 1, {"row": row + 1}),
        (col > 0, {"col": col - 1}),
        (col < ncol - 1, {"col": col + 1}),
    )
    for there, device in neighbours:
        @pl.when(there)
        def _():
            pl.semaphore_signal(barrier, inc=1, device_id=device, device_id_type=MESH)

    for copy in fetches[:4]:
        copy.wait()

    for axis, (rate, coef, length) in enumerate(((vrate, vcoef, rows), (hrate, hcoef, cols))):
        for h in range(halves):
            r = rate[:, h * LANES:(h + 1) * LANES]
            gain = jnp.sqrt(1.0 - jnp.exp(-2.0 * r))
            q = coef[:, h * LANES:(h + 1) * LANES] * gain
            ptab[axis, h] = jnp.exp(-r)
            qtab[axis, h] = q
            dtab[axis, h] = jnp.exp(-r * length)

    def fill_lead():
        for axis, (rate, length) in enumerate(((vrate, rows), (hrate, cols))):

            def fill(i, carry):
                for h in range(halves):
                    r = rate[:, h * LANES:(h + 1) * LANES]
                    q = qtab[axis, h]
                    for j in range(modes):
                        t = i * modes + j
                        power = jnp.exp(-r * (t + 1).astype(jnp.float32))
                        lead[axis, h, pl.ds(pl.multiple_of(t * modes, modes), modes), :] = q * power
                return carry

            lax.fori_loop(0, length // modes, fill, 0)

    def spread(tab, axis, h):
        block = tab[axis, h]
        return [jnp.broadcast_to(block[m:m + 1, :], (GROUP, LANES)) for m in range(modes)]

    def total(terms):
        while len(terms) > 1:
            terms = [a + b for a, b in zip(terms[::2], terms[1::2])] + terms[len(terms) & ~1:]
        return terms[0]

    def vcopy(g, i):
        part = pl.ds(i * (modes // PIECES), modes // PIECES)
        return pltpu.make_async_remote_copy(
            src_ref=vedge.at[g, part], dst_ref=vin.at[g, part],
            send_sem=vsend.at[g * PIECES + i], recv_sem=vrecv.at[g * PIECES + i],
            device_id={"row": row + 1}, device_id_type=MESH,
        )

    def hcopy(g, i):
        part = pl.ds(i * (modes // PIECES), modes // PIECES)
        return pltpu.make_async_remote_copy(
            src_ref=hedge.at[g, part], dst_ref=hin.at[g, part],
            send_sem=hsend.at[g * PIECES + i], recv_sem=hrecv.at[g * PIECES + i],
            device_id={"col": col + 1}, device_id_type=MESH,
        )

    def local(g):
        h, k = g // nk, g % nk

        @pl.when(h == 0)
        def _():
            fetch_image(k).wait()

        p, q = spread(ptab, 0, h), spread(qtab, 0, h)
        lane = pl.multiple_of(h * LANES, LANES)
        first = pl.multiple_of(k * GROUP, GROUP)

        def step(t, state):
            u = img[t, pl.ds(first, GROUP), pl.ds(lane, LANES)].astype(jnp.float32)
            state = tuple(p[m] * state[m] + u for m in range(modes))
            y = total([q[m] * state[m] for m in range(modes)])
            out[pl.ds(h * size + t * pitch + first, GROUP), :] = y
            return state

        zero = jnp.zeros((GROUP, LANES), jnp.float32)
        state = lax.fori_loop(0, rows, step, (zero,) * modes, unroll=4)
        for m in range(modes):
            vedge[g, m] = state[m]

    def enter(axis, g, h, place, count, edge, incoming, copy):
        for i in range(PIECES):
            @pl.when(place > 0)
            def _():
                copy(g, i).wait_recv()

            @pl.when(jnp.logical_and(place > 0, place < count - 1))
            def _():
                d = dtab[axis, h]
                for m in range(i * (modes // PIECES), (i + 1) * (modes // PIECES)):
                    edge[g, m] = jnp.broadcast_to(d[m:m + 1, :], (GROUP, LANES)) * incoming[g, m] + edge[g, m]
                copy(g, i).start()

    def enter_rows(g):
        enter(0, g, g // nk, row, nrow, vedge, vin, vcopy)

    def finish_rows(g):
        h, k = g // nk, g % nk
        first = pl.multiple_of(k * GROUP, GROUP)
        carried = [vin[g, m] for m in range(modes)]

        def correct(t, carry):
            at = pl.ds(h * size + t * pitch + first, GROUP)
            here = lead[0, h, pl.ds(pl.multiple_of(t * modes, modes), modes), :]
            y = out[at, :] + total([here[m:m + 1, :] * carried[m] for m in range(modes)])
            act = (0.5 * twice_gelu(y)).astype(jnp.bfloat16)
            out[at, :] = act.astype(jnp.float32)
            return carry

        lax.fori_loop(0, rows, correct, 0, unroll=8)
        p, q = spread(ptab, 1, h), spread(qtab, 1, h)

        def group(j, carry):
            c = h * nr + j
            base = h * size + j * (GROUP * pitch) + first

            def step(t, state):
                at = pl.ds(base + t, GROUP, stride=pitch)
                u = out[at, :]
                state = tuple(p[m] * state[m] + u for m in range(modes))
                out[at, :] = total([q[m] * state[m] for m in range(modes)])
                return state

            state = lax.fori_loop(0, GROUP, step, tuple(hedge[c, m] for m in range(modes)), unroll=4)
            for m in range(modes):
                hedge[c, m] = state[m]

            @pl.when(jnp.logical_and(k == nk - 1, jnp.logical_and(col == 0, ncol > 1)))
            def _():
                for i in range(PIECES):
                    hcopy(c, i).start()

            return carry

        lax.fori_loop(0, nr, group, 0)

    def enter_cols(c):
        enter(1, c, c // nr, col, ncol, hedge, hin, hcopy)

    def finish_cols(c):
        h, j = c // nr, c % nr

        @pl.when(col > 0)
        def _():
            carried = [hin[c, m] for m in range(modes)]
            base = h * size + j * (GROUP * pitch)

            def correct(t, carry):
                at = pl.ds(base + t, GROUP, stride=pitch)
                here = lead[1, h, pl.ds(pl.multiple_of(t * modes, modes), modes), :]
                out[at, :] = out[at, :] + total([here[m:m + 1, :] * carried[m] for m in range(modes)])
                return carry

            lax.fori_loop(0, cols, correct, 0, unroll=8)

    def mlp(i):
        line = jnp.concatenate(
            [
                jnp.concatenate([out[pl.ds(h * size + (i * BLOCK + r) * pitch, cols), :] for h in range(halves)], axis=1)
                for r in range(BLOCK)
            ],
            axis=0,
        )
        scale = lax.rsqrt(jnp.mean(line * line, axis=-1, keepdims=True) + 1e-06)
        normed = (line * scale).astype(jnp.bfloat16)
        pre = jnp.dot(normed, w_in[...], preferred_element_type=jnp.float32).astype(jnp.bfloat16)
        hidden = twice_gelu(pre)
        result = 0.5 * line + 0.25 * jnp.dot(hidden, w_out[...], preferred_element_type=jnp.float32)
        half[pl.ds(pl.multiple_of(i * (BLOCK * cols), BLOCK * cols), BLOCK * cols), :] = result.astype(half.dtype)
        store(i).start()

    def store(i):
        part = pl.ds(pl.multiple_of(i * (BLOCK * cols), BLOCK * cols), BLOCK * cols)
        return pltpu.make_async_copy(half.at[part], half_hbm.at[part], out_sem.at[i])

    hedge[...] = jnp.zeros_like(hedge)

    @pl.when(row == 0)
    def _():
        vin[...] = jnp.zeros_like(vin)

    pl.semaphore_wait(barrier, sum(jnp.where(there, 1, 0) for there, _ in neighbours))

    chunks = halves * nk
    strips = halves * nr

    def scan(s, carry):
        local(s)

        @pl.when(jnp.logical_and(row == 0, nrow > 1))
        def _():
            for i in range(PIECES):
                vcopy(s, i).start()

        @pl.when(jnp.logical_and(row == 1, s >= chunks - AHEAD))
        def _():
            enter_rows(s - (chunks - AHEAD))

        return carry

    lax.fori_loop(0, chunks, scan, 0)
    fill_lead()

    def main(g, carry):
        @pl.when(row != 1)
        def _():
            enter_rows(g)

        finish_rows(g)

        @pl.when(jnp.logical_and(row == 1, g + AHEAD < chunks))
        def _():
            enter_rows(g + AHEAD)

        @pl.when(g >= nk + col)
        def _():
            enter_cols(g - nk - col)
            finish_cols(g - nk - col)

        return carry

    lax.fori_loop(0, chunks, main, 0)
    early = (halves - 1) * nr

    def middle(c, carry):
        enter_cols(c)
        finish_cols(c)
        return carry

    lax.fori_loop(jnp.maximum(chunks - nk - col, 0), early, middle, 0)
    for copy in fetches[4:]:
        copy.wait()

    @pl.when(col < ncol - 1)
    def _():
        def relay(c, carry):
            enter_cols(c)
            return carry

        lax.fori_loop(early, strips, relay, 0)

    def last(c, carry):
        @pl.when(col == ncol - 1)
        def _():
            enter_cols(c)

        finish_cols(c)

        def block(i, carry):
            mlp(i)
            return carry

        per = GROUP // BLOCK
        lax.fori_loop((c - early) * per, (c - early + 1) * per, block, 0)
        return carry

    lax.fori_loop(early, strips, last, 0)

    def drain(g, carry):
        @pl.when(row < nrow - 1)
        def _():
            for i in range(PIECES):
                vcopy(g, i).wait_send()

        return carry

    lax.fori_loop(0, chunks, drain, 0)

    def drain_cols(g, carry):
        @pl.when(col < ncol - 1)
        def _():
            for i in range(PIECES):
                hcopy(g, i).wait_send()

        return carry

    lax.fori_loop(0, strips, drain_cols, 0)

    def stored(i, carry):
        store(i).wait()
        return carry

    lax.fori_loop(0, rows // BLOCK, stored, 0)


def on_device(nrow, ncol, image, vert_rate, vert_coef, horiz_rate, horiz_coef, w_in, w_out):
    rows, cols, channels = image.shape
    modes = vert_rate.shape[0]
    halves = channels // LANES
    chunks, strips = halves * (cols // GROUP), halves * (rows // GROUP)
    f32 = jnp.float32
    args = (image, vert_rate, vert_coef, horiz_rate, horiz_coef, w_in, w_out)
    half = pl.pallas_call(
        functools.partial(layer_kernel, nrow, ncol, rows, cols, modes, halves),
        out_shape=jax.ShapeDtypeStruct((rows * cols, channels), jnp.bfloat16),
        in_specs=[pl.BlockSpec(memory_space=pltpu.MemorySpace.HBM)] * len(args),
        out_specs=pl.BlockSpec(memory_space=pltpu.MemorySpace.HBM),
        scratch_shapes=[pltpu.VMEM(a.shape, a.dtype) for a in args] + [
            pltpu.VMEM((rows * cols, channels), jnp.bfloat16),
            pltpu.VMEM((halves * rows * (cols + 1), LANES), f32),
            pltpu.VMEM((2, halves, modes, LANES), f32),
            pltpu.VMEM((2, halves, modes, LANES), f32),
            pltpu.VMEM((2, halves, modes, LANES), f32),
            pltpu.VMEM((2, halves, max(rows, cols) * modes, LANES), f32),
            pltpu.VMEM((chunks, modes, GROUP, LANES), f32),
            pltpu.VMEM((chunks, modes, GROUP, LANES), f32),
            pltpu.VMEM((strips, modes, GROUP, LANES), f32),
            pltpu.VMEM((strips, modes, GROUP, LANES), f32),
            pltpu.SemaphoreType.DMA((chunks * PIECES,)),
            pltpu.SemaphoreType.DMA((chunks * PIECES,)),
            pltpu.SemaphoreType.DMA((strips * PIECES,)),
            pltpu.SemaphoreType.DMA((strips * PIECES,)),
            pltpu.SemaphoreType.DMA((cols // GROUP,)),
            pltpu.SemaphoreType.DMA((6,)),
            pltpu.SemaphoreType.DMA((rows // BLOCK,)),
        ],
        compiler_params=pltpu.CompilerParams(collective_id=0, has_side_effects=True, vmem_limit_bytes=67043328),
    )(*args)
    return (2.0 * half).reshape(rows, cols, channels)


def solution(mesh):
    placed = (P("row", "col", None), P(), P(), P(), P(), P(), P())
    return jax.shard_map(
        functools.partial(on_device, mesh.shape["row"], mesh.shape["col"]),
        mesh=mesh, in_specs=placed, out_specs=P("row", "col", None), check_vma=False,
    )
```

profile of v0, /device:TPU:30, one launch (start us, length us, event | category | flops | bytes accessed | tf_op | source)
XLA Modules:
  0.0 46.8 jit_solution(13145605669133287228)
XLA Ops:
  0.0 43.7 %shard_map.73 = bf16[4096,256]{1,0:T(8,128)(2,1)} custom-call(bf16[64,64,256]{2,1,0:T(8,128)(2,1)} %image_hbm.1, f32[8,256]{1,0:T(8,128)} %vrate_hbm.1, f32[8,256]{1,0:T(8,128)} %vcoef_hbm.1, f32[8,256]{1,0:T(8,128)} %hrate_hbm.1, f32[8,256]{1,0:T(8,128)} %hcoef_hbm.1, bf16[256,1024]{1,0:T(8,128)(2,1)} %w_in_hbm.1, bf16[1024,256]{1,0:T(8,128)(2,1)} %w_out_hbm.1), custom_call_target="tpu_custom_call" | custom-call | tf_op jit(solution)/shard_map/pallas_call | solution.py:355
  43.7 3.0 %broadcast_multiply_fusion = bf16[4096,256]{1,0:T(8,128)(2,1)} fusion(bf16[4096,256]{1,0:T(8,128)(2,1)} %shard_map.73), kind=kLoop, calls=%fused_computation | loop fusion | flops 1048576 | bytes 4194304 | tf_op jit(solution)/shard_map/mul | solution.py:381
where the time goes:
time: 47 us; the launch traced here: 46.8 us
  Pallas kernels  43.7 us (93%)
  other arithmetic  3.05 us (6%)
    pallas_call x1, Pallas kernels, on_device(): pl.pallas_call(functools.partial(layer_kernel, nrow, ncol, rows, cols, mo...  43.7 us
    mul x1, other arithmetic, on_device(): return (2.0 * half).reshape(rows, cols, channels)  3.05 us

commit v1 on v0

--- a/solution.py
+++ b/solution.py
@@ -23,8 +23,8 @@
 
 def layer_kernel(
     nrow, ncol, rows, cols, modes, halves,
-    image_hbm, vrate_hbm, vcoef_hbm, hrate_hbm, hcoef_hbm, w_in_hbm, w_out_hbm, half_hbm,
-    img, vrate, vcoef, hrate, hcoef, w_in, w_out, half, out,
+    image_hbm, vrate_hbm, vcoef_hbm, hrate_hbm, hcoef_hbm, w_in_hbm, w_out_hbm, half,
+    img, vrate, vcoef, hrate, hcoef, w_in, w_out, out,
     ptab, qtab, dtab, lead, vedge, vin, hedge, hin,
     vsend, vrecv, hsend, hrecv, img_sem, arg_sem, out_sem,
 ):
@@ -227,9 +227,8 @@
         normed = (line * scale).astype(jnp.bfloat16)
         pre = jnp.dot(normed, w_in[...], preferred_element_type=jnp.float32).astype(jnp.bfloat16)
         hidden = twice_gelu(pre)
-        result = 0.5 * line + 0.25 * jnp.dot(hidden, w_out[...], preferred_element_type=jnp.float32)
+        result = line + 0.5 * jnp.dot(hidden, w_out[...], preferred_element_type=jnp.float32)
         half[pl.ds(pl.multiple_of(i * (BLOCK * cols), BLOCK * cols), BLOCK * cols), :] = result.astype(half.dtype)
-        store(i).start()
 
     def store(i):
         part = pl.ds(pl.multiple_of(i * (BLOCK * cols), BLOCK * cols), BLOCK * cols)
@@ -338,11 +337,11 @@
 
     lax.fori_loop(0, strips, drain_cols, 0)
 
-    def stored(i, carry):
-        store(i).wait()
-        return carry
-
-    lax.fori_loop(0, rows // BLOCK, stored, 0)
+
+def emit(src, dst, sem):
+    copy = pltpu.make_async_copy(src, dst, sem.at[0])
+    copy.start()
+    copy.wait()
 
 
 def on_device(nrow, ncol, image, vert_rate, vert_coef, horiz_rate, horiz_coef, w_in, w_out):
@@ -354,11 +353,10 @@
     args = (image, vert_rate, vert_coef, horiz_rate, horiz_coef, w_in, w_out)
     half = pl.pallas_call(
         functools.partial(layer_kernel, nrow, ncol, rows, cols, modes, halves),
-        out_shape=jax.ShapeDtypeStruct((rows * cols, channels), jnp.bfloat16),
+        out_shape=pltpu.VMEM((rows * cols, channels), jnp.bfloat16),
         in_specs=[pl.BlockSpec(memory_space=pltpu.MemorySpace.HBM)] * len(args),
-        out_specs=pl.BlockSpec(memory_space=pltpu.MemorySpace.HBM),
+        out_specs=pl.BlockSpec(memory_space=pltpu.MemorySpace.VMEM),
         scratch_shapes=[pltpu.VMEM(a.shape, a.dtype) for a in args] + [
-            pltpu.VMEM((rows * cols, channels), jnp.bfloat16),
             pltpu.VMEM((halves * rows * (cols + 1), LANES), f32),
             pltpu.VMEM((2, halves, modes, LANES), f32),
             pltpu.VMEM((2, halves, modes, LANES), f32),
@@ -376,9 +374,16 @@
             pltpu.SemaphoreType.DMA((6,)),
             pltpu.SemaphoreType.DMA((rows // BLOCK,)),
         ],
-        compiler_params=pltpu.CompilerParams(collective_id=0, has_side_effects=True, vmem_limit_bytes=67043328),
+        compiler_params=pltpu.CompilerParams(collective_id=0, has_side_effects=True, vmem_limit_bytes=67043328 - rows * cols * channels * 2 - 4096),
     )(*args)
-    return (2.0 * half).reshape(rows, cols, channels)
+    full = pl.pallas_call(
+        emit, out_shape=jax.ShapeDtypeStruct((rows * cols, channels), jnp.bfloat16),
+        in_specs=[pl.BlockSpec(memory_space=pltpu.MemorySpace.VMEM)],
+        out_specs=pl.BlockSpec(memory_space=pltpu.MemorySpace.HBM),
+        scratch_shapes=[pltpu.SemaphoreType.DMA((1,))],
+        compiler_params=pltpu.CompilerParams(vmem_limit_bytes=1000000),
+    )(half)
+    return full.reshape(rows, cols, channels)
 
 
 def solution(mesh):

time: 47 us -> 44.6 us (0.949)
  other arithmetic: 3.05 us -> 0 us
  Pallas kernels: 43.7 us -> 44.4 us
    mul x1 -> x0, other arithmetic: 3.05 us -> none  [on_device(): return (2.0 * half).reshape(rows, cols, channels)]
    pallas_call x0 -> x1, Pallas kernels: none -> 1.33 us  [on_device(): pl.pallas_call(emit, out_shape=jax.ShapeDtypeStruct((rows * cols, channel...]
    pallas_call x1, Pallas kernels: 43.7 us -> 43 us  [on_device(): pl.pallas_call(functools.partial(layer_kernel, nrow, ncol, rows, cols, mo...]
where the time goes in v1:
time: 44.6 us; the launch traced here: 44.4 us
  Pallas kernels  44.4 us (100%)
    pallas_call x1, Pallas kernels, on_device(): pl.pallas_call(functools.partial(layer_kernel, nrow, ncol, rows, cols, mo...  43 us
    pallas_call x1, Pallas kernels, on_device(): pl.pallas_call(emit, out_shape=jax.ShapeDtypeStruct((rows * cols, channel...  1.33 us

profile of v1, /device:TPU:30, one launch (start us, length us, event | category | flops | bytes accessed | tf_op | source)
XLA Modules:
  0.0 44.4 jit_solution(15775957676348381242)
XLA Ops:
  0.0 43.0 %shard_map.73.src = bf16[4096,256]{1,0:T(8,128)(2,1)S(1)} custom-call(bf16[64,64,256]{2,1,0:T(8,128)(2,1)} %image_hbm.1, f32[8,256]{1,0:T(8,128)} %vrate_hbm.1, f32[8,256]{1,0:T(8,128)} %vcoef_hbm.1, f32[8,256]{1,0:T(8,128)} %hrate_hbm.1, f32[8,256]{1,0:T(8,128)} %hcoef_hbm.1, bf16[256,1024]{1,0:T(8,128)(2,1)} %w_in_hbm.1, bf16[1024,256]{1,0:T(8,128)(2,1)} %w_out_hbm.1), custom_call_target="tpu_custom_call" | custom-call | tf_op jit(solution)/shard_map/pallas_call | solution.py:354
  43.1 1.3 %shard_map.74 = bf16[4096,256]{1,0:T(8,128)(2,1)} custom-call(bf16[4096,256]{1,0:T(8,128)(2,1)S(1)} %shard_map.73.src), custom_call_target="tpu_custom_call" | custom-call | tf_op jit(solution)/shard_map/pallas_call | solution.py:379

commit v2 on v1

--- a/solution.py
+++ b/solution.py
@@ -10,7 +10,7 @@
 LANES = 128
 GROUP = 16
 BLOCK = 16
-AHEAD = 3
+AHEAD = 2
 PIECES = 2
 MESH = pl.DeviceIdType.MESH
 C0 = 0.7978845608028654
@@ -25,8 +25,8 @@
     nrow, ncol, rows, cols, modes, halves,
     image_hbm, vrate_hbm, vcoef_hbm, hrate_hbm, hcoef_hbm, w_in_hbm, w_out_hbm, half,
     img, vrate, vcoef, hrate, hcoef, w_in, w_out, out,
-    ptab, qtab, dtab, lead, vedge, vin, hedge, hin,
-    vsend, vrecv, hsend, hrecv, img_sem, arg_sem, out_sem,
+    ptab, qtab, vdt, vdp, hdt, lead, vtot, vin, vpre, hedge, hpart, hsum, hin, hcar,
+    vsend, vrecv, asend, arecv, csend, crecv, fsend, frecv, img_sem, arg_sem,
 ):
     row = lax.axis_index("row")
     col = lax.axis_index("col")
@@ -34,6 +34,13 @@
     nr = rows // GROUP
     pitch = cols + 1
     size = rows * pitch
+    steps = row_steps(nrow)
+    pair = pair_of(ncol)
+    core, z, nz = col % pair, col // pair, ncol // pair
+    chunks = halves * nk
+    strips = halves * nr
+    early = (halves - 1) * nr
+    both = jnp.logical_and
 
     def fetch_image(k):
         part = pl.ds(pl.multiple_of(k * GROUP, GROUP), GROUP)
@@ -53,13 +60,23 @@
     for copy in fetches[4:]:
         copy.start()
 
+    def bit_of(s):
+        return (row // (1 << s)) % 2
+
+    def row_partner(s):
+        return row + (1 << s) * (1 - 2 * bit_of(s))
+
+    def later(s):
+        return row // (1 << s) != (nrow >> s) - 1
+
     barrier = pltpu.get_barrier_semaphore()
-    neighbours = (
-        (row > 0, {"row": row - 1}),
-        (row < nrow - 1, {"row": row + 1}),
-        (col > 0, {"col": col - 1}),
-        (col < ncol - 1, {"col": col + 1}),
-    )
+    always = row >= 0
+    neighbours = [(always, {"row": row_partner(s)}) for s in range(steps)]
+    if pair == 2:
+        neighbours.append((always, {"col": col + 1 - 2 * core}))
+    if nz > 1:
+        neighbours.append((z > 0, {"col": col - pair}))
+        neighbours.append((z < nz - 1, {"col": col + pair}))
     for there, device in neighbours:
         @pl.when(there)
         def _():
@@ -68,14 +85,21 @@
     for copy in fetches[:4]:
         copy.wait()
 
-    for axis, (rate, coef, length) in enumerate(((vrate, vcoef, rows), (hrate, hcoef, cols))):
+    for axis, (rate, coef) in enumerate(((vrate, vcoef), (hrate, hcoef))):
         for h in range(halves):
             r = rate[:, h * LANES:(h + 1) * LANES]
             gain = jnp.sqrt(1.0 - jnp.exp(-2.0 * r))
-            q = coef[:, h * LANES:(h + 1) * LANES] * gain
             ptab[axis, h] = jnp.exp(-r)
-            qtab[axis, h] = q
-            dtab[axis, h] = jnp.exp(-r * length)
+            qtab[axis, h] = coef[:, h * LANES:(h + 1) * LANES] * gain
+
+    for h in range(halves):
+        r = vrate[:, h * LANES:(h + 1) * LANES]
+        for s in range(steps):
+            vdt[s, h] = jnp.exp(-r * (rows << s))
+            vdp[s, h] = jnp.exp(-r * (rows * (row % (1 << s))).astype(jnp.float32))
+        r = hrate[:, h * LANES:(h + 1) * LANES]
+        hdt[0, h] = jnp.exp(-r * cols)
+        hdt[1, h] = jnp.exp(-r * (cols * pair))
 
     def fill_lead():
         for axis, (rate, length) in enumerate(((vrate, rows), (hrate, cols))):
@@ -101,21 +125,39 @@
             terms = [a + b for a, b in zip(terms[::2], terms[1::2])] + terms[len(terms) & ~1:]
         return terms[0]
 
-    def vcopy(g, i):
+    def span(i):
+        return range(i * (modes // PIECES), (i + 1) * (modes // PIECES))
+
+    def vcopy(s, g, i):
         part = pl.ds(i * (modes // PIECES), modes // PIECES)
         return pltpu.make_async_remote_copy(
-            src_ref=vedge.at[g, part], dst_ref=vin.at[g, part],
-            send_sem=vsend.at[g * PIECES + i], recv_sem=vrecv.at[g * PIECES + i],
-            device_id={"row": row + 1}, device_id_type=MESH,
+            src_ref=vtot.at[s, g, part], dst_ref=vin.at[s, g, part],
+            send_sem=vsend.at[s, g * PIECES + i], recv_sem=vrecv.at[s, g * PIECES + i],
+            device_id={"row": row_partner(s)}, device_id_type=MESH,
         )
 
-    def hcopy(g, i):
+    def join_copy(c):
+        return pltpu.make_async_remote_copy(
+            src_ref=hedge.at[c], dst_ref=hpart.at[c], send_sem=asend.at[c], recv_sem=arecv.at[c],
+            device_id={"col": col + 1 - 2 * core}, device_id_type=MESH,
+        )
+
+    def chain_copy(c, i):
         part = pl.ds(i * (modes // PIECES), modes // PIECES)
         return pltpu.make_async_remote_copy(
-            src_ref=hedge.at[g, part], dst_ref=hin.at[g, part],
-            send_sem=hsend.at[g * PIECES + i], recv_sem=hrecv.at[g * PIECES + i],
-            device_id={"col": col + 1}, device_id_type=MESH,
+            src_ref=hsum.at[c, part], dst_ref=hin.at[c, part],
+            send_sem=csend.at[c * PIECES + i], recv_sem=crecv.at[c * PIECES + i],
+            device_id={"col": col + pair}, device_id_type=MESH,
         )
+
+    def forward_copy(src, c):
+        return pltpu.make_async_remote_copy(
+            src_ref=src.at[c], dst_ref=hin.at[c], send_sem=fsend.at[c], recv_sem=frecv.at[c],
+            device_id={"col": col + 1 - 2 * core}, device_id_type=MESH,
+        )
+
+    def owner(c):
+        return c % pair == core
 
     def local(g):
         h, k = g // nk, g % nk
@@ -138,28 +180,39 @@
         zero = jnp.zeros((GROUP, LANES), jnp.float32)
         state = lax.fori_loop(0, rows, step, (zero,) * modes, unroll=4)
         for m in range(modes):
-            vedge[g, m] = state[m]
-
-    def enter(axis, g, h, place, count, edge, incoming, copy):
+            vtot[0, g, m] = state[m]
+
+    def decay(tab, s, h, m):
+        return jnp.broadcast_to(tab[s, h][m:m + 1, :], (GROUP, LANES))
+
+    def exchange(s, g):
+        h = g // nk
+        bit = bit_of(s)
+        onward = later(s + 1)
         for i in range(PIECES):
-            @pl.when(place > 0)
-            def _():
-                copy(g, i).wait_recv()
-
-            @pl.when(jnp.logical_and(place > 0, place < count - 1))
-            def _():
-                d = dtab[axis, h]
-                for m in range(i * (modes // PIECES), (i + 1) * (modes // PIECES)):
-                    edge[g, m] = jnp.broadcast_to(d[m:m + 1, :], (GROUP, LANES)) * incoming[g, m] + edge[g, m]
-                copy(g, i).start()
-
-    def enter_rows(g):
-        enter(0, g, g // nk, row, nrow, vedge, vin, vcopy)
+            @pl.when(jnp.logical_or(bit == 1, onward))
+            def _():
+                vcopy(s, g, i).wait_recv()
+
+            if s + 1 < steps:
+                @pl.when(onward)
+                def _():
+                    for m in span(i):
+                        mine, theirs = vtot[s, g, m], vin[s, g, m]
+                        older = jnp.where(bit == 0, mine, theirs)
+                        newer = jnp.where(bit == 0, theirs, mine)
+                        vtot[s + 1, g, m] = decay(vdt, s, h, m) * older + newer
+                    vcopy(s + 1, g, i).start()
+
+            @pl.when(bit == 1)
+            def _():
+                for m in span(i):
+                    vpre[g, m] = decay(vdp, s, h, m) * vin[s, g, m] + vpre[g, m]
 
     def finish_rows(g):
         h, k = g // nk, g % nk
         first = pl.multiple_of(k * GROUP, GROUP)
-        carried = [vin[g, m] for m in range(modes)]
+        carried = [vpre[g, m] for m in range(modes)]
 
         def correct(t, carry):
             at = pl.ds(h * size + t * pitch + first, GROUP)
@@ -187,24 +240,90 @@
             for m in range(modes):
                 hedge[c, m] = state[m]
 
-            @pl.when(jnp.logical_and(k == nk - 1, jnp.logical_and(col == 0, ncol > 1)))
-            def _():
-                for i in range(PIECES):
-                    hcopy(c, i).start()
+            if pair == 2:
+                @pl.when(both(k == nk - 1, jnp.logical_not(owner(c))))
+                def _():
+                    join_copy(c).start()
 
             return carry
 
         lax.fori_loop(0, nr, group, 0)
 
-    def enter_cols(c):
-        enter(1, c, c // nr, col, ncol, hedge, hin, hcopy)
+    def join(c):
+        h = c // nr
+
+        @pl.when(owner(c))
+        def _():
+            if pair == 2:
+                join_copy(c).wait_recv()
+            for m in range(modes):
+                mine = hedge[c, m]
+                if pair == 2:
+                    theirs = hpart[c, m]
+                    older = jnp.where(core == 0, mine, theirs)
+                    newer = jnp.where(core == 0, theirs, mine)
+                    mine = decay(hdt, 0, h, m) * older + newer
+                hsum[c, m] = mine
+            if nz > 1:
+                @pl.when(z == 0)
+                def _():
+                    for i in range(PIECES):
+                        chain_copy(c, i).start()
+            if pair == 2:
+                @pl.when(col == 0)
+                def _():
+                    forward_copy(hedge, c).start()
+
+    def enter(c):
+        h = c // nr
+
+        @pl.when(both(owner(c), z > 0))
+        def _():
+            for i in range(PIECES):
+                chain_copy(c, i).wait_recv()
+
+                @pl.when(z < nz - 1)
+                def _():
+                    for m in span(i):
+                        hsum[c, m] = decay(hdt, 1, h, m) * hin[c, m] + hsum[c, m]
+                    chain_copy(c, i).start()
+
+            if pair == 2:
+                @pl.when(core == 0)
+                def _():
+                    for m in range(modes):
+                        hpart[c, m] = decay(hdt, 0, h, m) * hin[c, m] + hedge[c, m]
+                    forward_copy(hpart, c).start()
+                    for m in range(modes):
+                        hcar[c, m] = hin[c, m]
+
+                @pl.when(core == 1)
+                def _():
+                    forward_copy(hin, c).start()
+                    for m in range(modes):
+                        hcar[c, m] = decay(hdt, 0, h, m) * hin[c, m] + hpart[c, m]
+            else:
+                for m in range(modes):
+                    hcar[c, m] = hin[c, m]
+
+        if pair == 2:
+            @pl.when(both(owner(c), col == 1))
+            def _():
+                for m in range(modes):
+                    hcar[c, m] = hpart[c, m]
+
+            @pl.when(both(jnp.logical_not(owner(c)), col > 0))
+            def _():
+                forward_copy(hin, c).wait_recv()
+                for m in range(modes):
+                    hcar[c, m] = hin[c, m]
 
     def finish_cols(c):
         h, j = c // nr, c % nr
 
         @pl.when(col > 0)
         def _():
-            carried = [hin[c, m] for m in range(modes)]
+            carried = [hcar[c, m] for m in range(modes)]
             base = h * size + j * (GROUP * pitch)
 
             def correct(t, carry):
@@ -230,32 +349,22 @@
         result = line + 0.5 * jnp.dot(hidden, w_out[...], preferred_element_type=jnp.float32)
         half[pl.ds(pl.multiple_of(i * (BLOCK * cols), BLOCK * cols), BLOCK * cols), :] = result.astype(half.dtype)
 
-    def store(i):
-        part = pl.ds(pl.multiple_of(i * (BLOCK * cols), BLOCK * cols), BLOCK * cols)
-        return pltpu.make_async_copy(half.at[part], half_hbm.at[part], out_sem.at[i])
-
     hedge[...] = jnp.zeros_like(hedge)
-
-    @pl.when(row == 0)
-    def _():
-        vin[...] = jnp.zeros_like(vin)
+    vpre[...] = jnp.zeros_like(vpre)
 
     pl.semaphore_wait(barrier, sum(jnp.where(there, 1, 0) for there, _ in neighbours))
-
-    chunks = halves * nk
-    strips = halves * nr
 
     def scan(s, carry):
         local(s)
-
-        @pl.when(jnp.logical_and(row == 0, nrow > 1))
-        def _():
-            for i in range(PIECES):
-                vcopy(s, i).start()
-
-        @pl.when(jnp.logical_and(row == 1, s >= chunks - AHEAD))
-        def _():
-            enter_rows(s - (chunks - AHEAD))
+        if steps:
+            @pl.when(later(0))
+            def _():
+                for i in range(PIECES):
+                    vcopy(0, s, i).start()
+
+            @pl.when(s >= chunks - AHEAD)
+            def _():
+                exchange(0, s - (chunks - AHEAD))
 
         return carry
 
@@ -263,79 +372,86 @@
     fill_lead()
 
     def main(g, carry):
-        @pl.when(row != 1)
-        def _():
-            enter_rows(g)
-
+        for s in range(1, steps):
+            exchange(s, g)
         finish_rows(g)
-
-        @pl.when(jnp.logical_and(row == 1, g + AHEAD < chunks))
-        def _():
-            enter_rows(g + AHEAD)
-
-        @pl.when(g >= nk + col)
-        def _():
-            enter_cols(g - nk - col)
-            finish_cols(g - nk - col)
+        if steps:
+            @pl.when(g + AHEAD < chunks)
+            def _():
+                exchange(0, g + AHEAD)
+
+        @pl.when(both(g % nk == 0, g > 0))
+        def _():
+            each(0, nr, lambda j: join((g // nk - 1) * nr + j))
 
         return carry
 
+    def each(first, last, act):
+        def go(c, carry):
+            act(c)
+            return carry
+
+        lax.fori_loop(first, last, go, 0)
+
     lax.fori_loop(0, chunks, main, 0)
-    early = (halves - 1) * nr
-
-    def middle(c, carry):
-        enter_cols(c)
-        finish_cols(c)
-        return carry
-
-    lax.fori_loop(jnp.maximum(chunks - nk - col, 0), early, middle, 0)
+    each(0, early, enter)
+    each(early, strips, join)
+    each(0, early, finish_cols)
     for copy in fetches[4:]:
         copy.wait()
 
-    @pl.when(col < ncol - 1)
+    def turn(n):
+        turns = nr // pair
+        return early + pair * (n % turns) + (core + n // turns) % pair
+
+    @pl.when(z < nz - 1)
     def _():
-        def relay(c, carry):
-            enter_cols(c)
-            return carry
-
-        lax.fori_loop(early, strips, relay, 0)
-
-    def last(c, carry):
-        @pl.when(col == ncol - 1)
-        def _():
-            enter_cols(c)
+        each(0, nr, lambda n: enter(turn(n)))
+
+    def last(n):
+        c = turn(n)
+
+        @pl.when(z == nz - 1)
+        def _():
+            enter(c)
 
         finish_cols(c)
-
-        def block(i, carry):
-            mlp(i)
-            return carry
-
         per = GROUP // BLOCK
-        lax.fori_loop((c - early) * per, (c - early + 1) * per, block, 0)
-        return carry
-
-    lax.fori_loop(early, strips, last, 0)
-
-    def drain(g, carry):
-        @pl.when(row < nrow - 1)
+        each((c - early) * per, (c - early + 1) * per, mlp)
+
+    each(0, nr, last)
+
+    for s in range(steps):
+        @pl.when(later(s))
+        def _():
+            each(0, chunks * PIECES, lambda n: vcopy(s, n // PIECES, n % PIECES).wait_send())
+
+    def drain(c):
+        @pl.when(both(owner(c), z < nz - 1))
         def _():
             for i in range(PIECES):
-                vcopy(g, i).wait_send()
-
-        return carry
-
-    lax.fori_loop(0, chunks, drain, 0)
-
-    def drain_cols(g, carry):
-        @pl.when(col < ncol - 1)
-        def _():
-            for i in range(PIECES):
-                hcopy(g, i).wait_send()
-
-        return carry
-
-    lax.fori_loop(0, strips, drain_cols, 0)
+                chain_copy(c, i).wait_send()
+
+        if pair == 2:
+            @pl.when(jnp.logical_not(owner(c)))
+            def _():
+                join_copy(c).wait_send()
+
+            @pl.when(both(owner(c), col != 1))
+            def _():
+                forward_copy(hin, c).wait_send()
+
+    each(0, strips, drain)
+
+
+def row_steps(nrow):
+    steps = nrow.bit_length() - 1
+    assert nrow == 1 << steps
+    return steps
+
+
+def pair_of(ncol):
+    return 2 if ncol % 2 == 0 else 1
 
 
 def emit(src, dst, sem):
@@ -349,6 +465,7 @@
     modes = vert_rate.shape[0]
     halves = channels // LANES
     chunks, strips = halves * (cols // GROUP), halves * (rows // GROUP)
+    steps = max(row_steps(nrow), 1)
     f32 = jnp.float32
     args = (image, vert_rate, vert_coef, horiz_rate, horiz_coef, w_in, w_out)
     half = pl.pallas_call(
@@ -360,19 +477,24 @@
             pltpu.VMEM((halves * rows * (cols + 1), LANES), f32),
             pltpu.VMEM((2, halves, modes, LANES), f32),
             pltpu.VMEM((2, halves, modes, LANES), f32),
+            pltpu.VMEM((steps, halves, modes, LANES), f32),
+            pltpu.VMEM((steps, halves, modes, LANES), f32),
             pltpu.VMEM((2, halves, modes, LANES), f32),
             pltpu.VMEM((2, halves, max(rows, cols) * modes, LANES), f32),
+            pltpu.VMEM((steps, chunks, modes, GROUP, LANES), f32),
+            pltpu.VMEM((steps, chunks, modes, GROUP, LANES), f32),
             pltpu.VMEM((chunks, modes, GROUP, LANES), f32),
-            pltpu.VMEM((chunks, modes, GROUP, LANES), f32),
-            pltpu.VMEM((strips, modes, GROUP, LANES), f32),
-            pltpu.VMEM((strips, modes, GROUP, LANES), f32),
-            pltpu.SemaphoreType.DMA((chunks * PIECES,)),
-            pltpu.SemaphoreType.DMA((chunks * PIECES,)),
+        ] + [pltpu.VMEM((strips, modes, GROUP, LANES), f32)] * 5 + [
+            pltpu.SemaphoreType.DMA((steps, chunks * PIECES)),
+            pltpu.SemaphoreType.DMA((steps, chunks * PIECES)),
+            pltpu.SemaphoreType.DMA((strips,)),
+            pltpu.SemaphoreType.DMA((strips,)),
             pltpu.SemaphoreType.DMA((strips * PIECES,)),
             pltpu.SemaphoreType.DMA((strips * PIECES,)),
+            pltpu.SemaphoreType.DMA((strips,)),
+            pltpu.SemaphoreType.DMA((strips,)),
             pltpu.SemaphoreType.DMA((cols // GROUP,)),
             pltpu.SemaphoreType.DMA((6,)),
-            pltpu.SemaphoreType.DMA((rows // BLOCK,)),
         ],
         compiler_params=pltpu.CompilerParams(collective_id=0, has_side_effects=True, vmem_limit_bytes=67043328 - rows * cols * channels * 2 - 4096),
     )(*args)

time: 44.6 us -> 42.6 us (0.955)
  the two profiles are of different devices: /device:TPU:30 before, /device:TPU:28 now
where the time goes in v2:
time: 42.6 us; the launch traced here: 42.4 us
  Pallas kernels  42.4 us (100%)
    pallas_call x1, Pallas kernels, on_device(): pl.pallas_call(functools.partial(layer_kernel, nrow, ncol, rows, cols, mo...  41.1 us
    pallas_call x1, Pallas kernels, on_device(): pl.pallas_call(emit, out_shape=jax.ShapeDtypeStruct((rows * cols, channel...  1.33 us

profile of v2, /device:TPU:28, one launch (start us, length us, event | category | flops | bytes accessed | tf_op | source)
XLA Modules:
  0.0 42.4 jit_solution(4366951548781047033)
XLA Ops:
  0.0 41.1 %shard_map.73.src = bf16[4096,256]{1,0:T(8,128)(2,1)S(1)} custom-call(bf16[64,64,256]{2,1,0:T(8,128)(2,1)} %image_hbm.1, f32[8,256]{1,0:T(8,128)} %vrate_hbm.1, f32[8,256]{1,0:T(8,128)} %vcoef_hbm.1, f32[8,256]{1,0:T(8,128)} %hrate_hbm.1, f32[8,256]{1,0:T(8,128)} %hcoef_hbm.1, bf16[256,1024]{1,0:T(8,128)(2,1)} %w_in_hbm.1, bf16[1024,256]{1,0:T(8,128)(2,1)} %w_out_hbm.1), custom_call_target="tpu_custom_call" | custom-call | tf_op jit(solution)/shard_map/pallas_call | solution.py:471
  41.1 1.3 %shard_map.74 = bf16[4096,256]{1,0:T(8,128)(2,1)} custom-call(bf16[4096,256]{1,0:T(8,128)(2,1)S(1)} %shard_map.73.src), custom_call_target="tpu_custom_call" | custom-call | tf_op jit(solution)/shard_map/pallas_call | solution.py:501

commit v3 on v2

--- a/solution.py
+++ b/solution.py
@@ -11,7 +11,8 @@
 GROUP = 16
 BLOCK = 16
 AHEAD = 2
-PIECES = 2
+PIECES = 1
+HOPS = 1
 MESH = pl.DeviceIdType.MESH
 C0 = 0.7978845608028654
 C1 = 0.7978845608028654 * 0.044715
@@ -25,7 +26,7 @@
     nrow, ncol, rows, cols, modes, halves,
     image_hbm, vrate_hbm, vcoef_hbm, hrate_hbm, hcoef_hbm, w_in_hbm, w_out_hbm, half,
     img, vrate, vcoef, hrate, hcoef, w_in, w_out, out,
-    ptab, qtab, vdt, vdp, hdt, lead, vtot, vin, vpre, hedge, hpart, hsum, hin, hcar,
+    ptab, qtab, vdt, vdp, hdt, lead, vtot, vin, vpre, hin, hedge, hpart, hsum, hfwd, hcar,
     vsend, vrecv, asend, arecv, csend, crecv, fsend, frecv, img_sem, arg_sem,
 ):
     row = lax.axis_index("row")
@@ -34,13 +35,35 @@
     nr = rows // GROUP
     pitch = cols + 1
     size = rows * pitch
-    steps = row_steps(nrow)
+    steps = log_two(nrow)
     pair = pair_of(ncol)
     core, z, nz = col % pair, col // pair, ncol // pair
     chunks = halves * nk
     strips = halves * nr
     early = (halves - 1) * nr
     both = jnp.logical_and
+
+    def bit_of(s):
+        return (row // (1 << s)) % 2
+
+    def row_partner(s):
+        return row + (1 << s) * (1 - 2 * bit_of(s))
+
+    def later(s):
+        return row // (1 << s) != (nrow >> s) - 1
+
+    barrier = pltpu.get_barrier_semaphore()
+    always = row >= 0
+    neighbours = [(always, {"row": row_partner(s)}) for s in range(steps)]
+    if pair == 2:
+        neighbours.append((always, {"col": col + 1 - 2 * core}))
+    if nz > 1:
+        neighbours.append((z > 0, {"col": col - pair}))
+        neighbours.append((z < nz - 1, {"col": col + pair}))
+    for there, device in neighbours:
+        @pl.when(there)
+        def _():
+            pl.semaphore_signal(barrier, inc=1, device_id=device, device_id_type=MESH)
 
     def fetch_image(k):
         part = pl.ds(pl.multiple_of(k * GROUP, GROUP), GROUP)
@@ -57,30 +80,6 @@
         copy.start()
     for k in range(nk):
         fetch_image(k).start()
-    for copy in fetches[4:]:
-        copy.start()
-
-    def bit_of(s):
-        return (row // (1 << s)) % 2
-
-    def row_partner(s):
-        return row + (1 << s) * (1 - 2 * bit_of(s))
-
-    def later(s):
-        return row // (1 << s) != (nrow >> s) - 1
-
-    barrier = pltpu.get_barrier_semaphore()
-    always = row >= 0
-    neighbours = [(always, {"row": row_partner(s)}) for s in range(steps)]
-    if pair == 2:
-        neighbours.append((always, {"col": col + 1 - 2 * core}))
-    if nz > 1:
-        neighbours.append((z > 0, {"col": col - pair}))
-        neighbours.append((z < nz - 1, {"col": col + pair}))
-    for there, device in neighbours:
-        @pl.when(there)
-        def _():
-            pl.semaphore_signal(barrier, inc=1, device_id=device, device_id_type=MESH)
 
     for copy in fetches[:4]:
         copy.wait()
@@ -142,17 +141,17 @@
             device_id={"col": col + 1 - 2 * core}, device_id_type=MESH,
         )
 
-    def chain_copy(c, i):
-        part = pl.ds(i * (modes // PIECES), modes // PIECES)
+    def hop_copy(c, i):
+        part = pl.ds(i * (modes // HOPS), modes // HOPS)
         return pltpu.make_async_remote_copy(
             src_ref=hsum.at[c, part], dst_ref=hin.at[c, part],
-            send_sem=csend.at[c * PIECES + i], recv_sem=crecv.at[c * PIECES + i],
+            send_sem=csend.at[c * HOPS + i], recv_sem=crecv.at[c * HOPS + i],
             device_id={"col": col + pair}, device_id_type=MESH,
         )
 
     def forward_copy(src, c):
         return pltpu.make_async_remote_copy(
-            src_ref=src.at[c], dst_ref=hin.at[c], send_sem=fsend.at[c], recv_sem=frecv.at[c],
+            src_ref=src.at[c], dst_ref=hfwd.at[c], send_sem=fsend.at[c], recv_sem=frecv.at[c],
             device_id={"col": col + 1 - 2 * core}, device_id_type=MESH,
         )
 
@@ -165,6 +164,11 @@
         @pl.when(h == 0)
         def _():
             fetch_image(k).wait()
+
+        @pl.when(g == nk)
+        def _():
+            for copy in fetches[4:]:
+                copy.start()
 
         p, q = spread(ptab, 0, h), spread(qtab, 0, h)
         lane = pl.multiple_of(h * LANES, LANES)
@@ -178,7 +182,7 @@
             return state
 
         zero = jnp.zeros((GROUP, LANES), jnp.float32)
-        state = lax.fori_loop(0, rows, step, (zero,) * modes, unroll=4)
+        state = lax.fori_loop(0, rows, step, (zero,) * modes, unroll=16)
         for m in range(modes):
             vtot[0, g, m] = state[m]
 
@@ -222,7 +226,7 @@
             out[at, :] = act.astype(jnp.float32)
             return carry
 
-        lax.fori_loop(0, rows, correct, 0, unroll=8)
+        lax.fori_loop(0, rows, correct, 0, unroll=16)
         p, q = spread(ptab, 1, h), spread(qtab, 1, h)
 
         def group(j, carry):
@@ -236,7 +240,7 @@
                 out[at, :] = total([q[m] * state[m] for m in range(modes)])
                 return state
 
-            state = lax.fori_loop(0, GROUP, step, tuple(hedge[c, m] for m in range(modes)), unroll=4)
+            state = lax.fori_loop(0, GROUP, step, tuple(hedge[c, m] for m in range(modes)), unroll=16)
             for m in range(modes):
                 hedge[c, m] = state[m]
 
@@ -267,8 +271,8 @@
             if nz > 1:
                 @pl.when(z == 0)
                 def _():
-                    for i in range(PIECES):
-                        chain_copy(c, i).start()
+                    for i in range(HOPS):
+                        hop_copy(c, i).start()
             if pair == 2:
                 @pl.when(col == 0)
                 def _():
@@ -279,14 +283,15 @@
 
         @pl.when(both(owner(c), z > 0))
         def _():
-            for i in range(PIECES):
-                chain_copy(c, i).wait_recv()
+            for i in range(HOPS):
+                part = range(i * (modes // HOPS), (i + 1) * (modes // HOPS))
+                hop_copy(c, i).wait_recv()
 
                 @pl.when(z < nz - 1)
                 def _():
-                    for m in span(i):
+                    for m in part:
                         hsum[c, m] = decay(hdt, 1, h, m) * hin[c, m] + hsum[c, m]
-                    chain_copy(c, i).start()
+                    hop_copy(c, i).start()
 
             if pair == 2:
                 @pl.when(core == 0)
@@ -316,7 +321,7 @@
             def _():
                 forward_copy(hin, c).wait_recv()
                 for m in range(modes):
-                    hcar[c, m] = hin[c, m]
+                    hcar[c, m] = hfwd[c, m]
 
     def finish_cols(c):
         h, j = c // nr, c % nr
@@ -332,7 +337,7 @@
                 out[at, :] = out[at, :] + total([here[m:m + 1, :] * carried[m] for m in range(modes)])
                 return carry
 
-            lax.fori_loop(0, cols, correct, 0, unroll=8)
+            lax.fori_loop(0, cols, correct, 0, unroll=16)
 
     def mlp(i):
         line = jnp.concatenate(
@@ -352,10 +357,13 @@
     hedge[...] = jnp.zeros_like(hedge)
     vpre[...] = jnp.zeros_like(vpre)
 
-    pl.semaphore_wait(barrier, sum(jnp.where(there, 1, 0) for there, _ in neighbours))
-
     def scan(s, carry):
         local(s)
+
+        @pl.when(s == 0)
+        def _():
+            pl.semaphore_wait(barrier, sum(jnp.where(there, 1, 0) for there, _ in neighbours))
+
         if steps:
             @pl.when(later(0))
             def _():
@@ -394,19 +402,20 @@
         lax.fori_loop(first, last, go, 0)
 
     lax.fori_loop(0, chunks, main, 0)
-    each(0, early, enter)
-    each(early, strips, join)
-    each(0, early, finish_cols)
+
+    def turn(n):
+        turns = nr // pair
+        return (n // nr) * nr + pair * (n % turns) + (core + (n % nr) // turns) % pair
+
+    each(0, early, lambda n: enter(turn(n)))
+    each(early, strips, lambda n: join(turn(n)))
+    each(0, early, lambda n: finish_cols(turn(n)))
     for copy in fetches[4:]:
         copy.wait()
 
-    def turn(n):
-        turns = nr // pair
-        return early + pair * (n % turns) + (core + n // turns) % pair
-
     @pl.when(z < nz - 1)
     def _():
-        each(0, nr, lambda n: enter(turn(n)))
+        each(early, strips, lambda n: enter(turn(n)))
 
     def last(n):
         c = turn(n)
@@ -419,7 +428,7 @@
         per = GROUP // BLOCK
         each((c - early) * per, (c - early + 1) * per, mlp)
 
-    each(0, nr, last)
+    each(early, strips, last)
 
     for s in range(steps):
         @pl.when(later(s))
@@ -427,10 +436,11 @@
             each(0, chunks * PIECES, lambda n: vcopy(s, n // PIECES, n % PIECES).wait_send())
 
     def drain(c):
-        @pl.when(both(owner(c), z < nz - 1))
-        def _():
-            for i in range(PIECES):
-                chain_copy(c, i).wait_send()
+        if nz > 1:
+            @pl.when(both(owner(c), z < nz - 1))
+            def _():
+                for i in range(HOPS):
+                    hop_copy(c, i).wait_send()
 
         if pair == 2:
             @pl.when(jnp.logical_not(owner(c)))
@@ -444,9 +454,9 @@
     each(0, strips, drain)
 
 
-def row_steps(nrow):
-    steps = nrow.bit_length() - 1
-    assert nrow == 1 << steps
+def log_two(count):
+    steps = count.bit_length() - 1
+    assert count == 1 << steps
     return steps
 
 
@@ -465,7 +475,7 @@
     modes = vert_rate.shape[0]
     halves = channels // LANES
     chunks, strips = halves * (cols // GROUP), halves * (rows // GROUP)
-    steps = max(row_steps(nrow), 1)
+    steps = max(log_two(nrow), 1)
     f32 = jnp.float32
     args = (image, vert_rate, vert_coef, horiz_rate, horiz_coef, w_in, w_out)
     half = pl.pallas_call(
@@ -484,13 +494,13 @@
             pltpu.VMEM((steps, chunks, modes, GROUP, LANES), f32),
             pltpu.VMEM((steps, chunks, modes, GROUP, LANES), f32),
             pltpu.VMEM((chunks, modes, GROUP, LANES), f32),
-        ] + [pltpu.VMEM((strips, modes, GROUP, LANES), f32)] * 5 + [
+        ] + [pltpu.VMEM((strips, modes, GROUP, LANES), f32)] * 6 + [
             pltpu.SemaphoreType.DMA((steps, chunks * PIECES)),
             pltpu.SemaphoreType.DMA((steps, chunks * PIECES)),
             pltpu.SemaphoreType.DMA((strips,)),
             pltpu.SemaphoreType.DMA((strips,)),
-            pltpu.SemaphoreType.DMA((strips * PIECES,)),
-            pltpu.SemaphoreType.DMA((strips * PIECES,)),
+            pltpu.SemaphoreType.DMA((strips * HOPS,)),
+            pltpu.SemaphoreType.DMA((strips * HOPS,)),
             pltpu.SemaphoreType.DMA((strips,)),
             pltpu.SemaphoreType.DMA((strips,)),
             pltpu.SemaphoreType.DMA((cols // GROUP,)),

time: 42.6 us -> 39.7 us (0.932)
  Pallas kernels: 42.4 us -> 39.5 us
    pallas_call x1, Pallas kernels: 41.1 us -> 38.1 us  [on_device(): pl.pallas_call(functools.partial(layer_kernel, nrow, ncol, rows, cols, mo...]
where the time goes in v3:
time: 39.7 us; the launch traced here: 39.5 us
  Pallas kernels  39.5 us (99%)
    pallas_call x1, Pallas kernels, on_device(): pl.pallas_call(functools.partial(layer_kernel, nrow, ncol, rows, cols, mo...  38.1 us
    pallas_call x1, Pallas kernels, on_device(): pl.pallas_call(emit, out_shape=jax.ShapeDtypeStruct((rows * cols, channel...  1.33 us

profile of v3, /device:TPU:28, one launch (start us, length us, event | category | flops | bytes accessed | tf_op | source)
XLA Modules:
  0.0 39.5 jit_solution(12661845335791110234)
XLA Ops:
  0.0 38.1 %shard_map.73.src = bf16[4096,256]{1,0:T(8,128)(2,1)S(1)} custom-call(bf16[64,64,256]{2,1,0:T(8,128)(2,1)} %image_hbm.1, f32[8,256]{1,0:T(8,128)} %vrate_hbm.1, f32[8,256]{1,0:T(8,128)} %vcoef_hbm.1, f32[8,256]{1,0:T(8,128)} %hrate_hbm.1, f32[8,256]{1,0:T(8,128)} %hcoef_hbm.1, bf16[256,1024]{1,0:T(8,128)(2,1)} %w_in_hbm.1, bf16[1024,256]{1,0:T(8,128)(2,1)} %w_out_hbm.1), custom_call_target="tpu_custom_call" | custom-call | tf_op jit(solution)/shard_map/pallas_call | solution.py:481
  38.1 1.3 %shard_map.74 = bf16[4096,256]{1,0:T(8,128)(2,1)} custom-call(bf16[4096,256]{1,0:T(8,128)(2,1)S(1)} %shard_map.73.src), custom_call_target="tpu_custom_call" | custom-call | tf_op jit(solution)/shard_map/pallas_call | solution.py:511

commit v4 on v3

--- a/solution.py
+++ b/solution.py
@@ -10,9 +10,10 @@
 LANES = 128
 GROUP = 16
 BLOCK = 16
-AHEAD = 2
+AHEAD = 3
 PIECES = 1
 HOPS = 1
+PARTS = 8
 MESH = pl.DeviceIdType.MESH
 C0 = 0.7978845608028654
 C1 = 0.7978845608028654 * 0.044715
@@ -89,7 +90,7 @@
             r = rate[:, h * LANES:(h + 1) * LANES]
             gain = jnp.sqrt(1.0 - jnp.exp(-2.0 * r))
             ptab[axis, h] = jnp.exp(-r)
-            qtab[axis, h] = coef[:, h * LANES:(h + 1) * LANES] * gain
+            qtab[axis, h] = coef[:, h * LANES:(h + 1) * LANES] * (gain if axis == 0 else 0.5 * gain)
 
     for h in range(halves):
         r = vrate[:, h * LANES:(h + 1) * LANES]
@@ -222,7 +223,7 @@
             at = pl.ds(h * size + t * pitch + first, GROUP)
             here = lead[0, h, pl.ds(pl.multiple_of(t * modes, modes), modes), :]
             y = out[at, :] + total([here[m:m + 1, :] * carried[m] for m in range(modes)])
-            act = (0.5 * twice_gelu(y)).astype(jnp.bfloat16)
+            act = twice_gelu(y).astype(jnp.bfloat16)
             out[at, :] = act.astype(jnp.float32)
             return carry
 
@@ -465,9 +466,15 @@
 
 
 def emit(src, dst, sem):
-    copy = pltpu.make_async_copy(src, dst, sem.at[0])
-    copy.start()
-    copy.wait()
+    rows = src.shape[0] // PARTS
+    copies = [
+        pltpu.make_async_copy(src.at[pl.ds(i * rows, rows)], dst.at[pl.ds(i * rows, rows)], sem.at[i])
+        for i in range(PARTS)
+    ]
+    for copy in copies:
+        copy.start()
+    for copy in copies:
+        copy.wait()
 
 
 def on_device(nrow, ncol, image, vert_rate, vert_coef, horiz_rate, horiz_coef, w_in, w_out):
@@ -512,7 +519,7 @@
         emit, out_shape=jax.ShapeDtypeStruct((rows * cols, channels), jnp.bfloat16),
         in_specs=[pl.BlockSpec(memory_space=pltpu.MemorySpace.VMEM)],
         out_specs=pl.BlockSpec(memory_space=pltpu.MemorySpace.HBM),
-        scratch_shapes=[pltpu.SemaphoreType.DMA((1,))],
+        scratch_shapes=[pltpu.SemaphoreType.DMA((PARTS,))],
         compiler_params=pltpu.CompilerParams(vmem_limit_bytes=1000000),
     )(half)
     return full.reshape(rows, cols, channels)

time: 39.7 us -> 39.2 us (0.987)
  Pallas kernels: 39.5 us -> 39 us
    pallas_call x1, Pallas kernels: 38.1 us -> 37.6 us  [on_device(): pl.pallas_call(functools.partial(layer_kernel, nrow, ncol, rows, cols, mo...]
where the time goes in v4:
time: 39.2 us; the launch traced here: 39 us
  Pallas kernels  39 us (99%)
    pallas_call x1, Pallas kernels, on_device(): pl.pallas_call(functools.partial(layer_kernel, nrow, ncol, rows, cols, mo...  37.6 us
    pallas_call x1, Pallas kernels, on_device(): pl.pallas_call(emit, out_shape=jax.ShapeDtypeStruct((rows * cols, channel...  1.38 us

profile of v4, /device:TPU:28, one launch (start us, length us, event | category | flops | bytes accessed | tf_op | source)
XLA Modules:
  0.0 39.0 jit_solution(906043389996759778)
XLA Ops:
  0.0 37.6 %shard_map.73.src = bf16[4096,256]{1,0:T(8,128)(2,1)S(1)} custom-call(bf16[64,64,256]{2,1,0:T(8,128)(2,1)} %image_hbm.1, f32[8,256]{1,0:T(8,128)} %vrate_hbm.1, f32[8,256]{1,0:T(8,128)} %vcoef_hbm.1, f32[8,256]{1,0:T(8,128)} %hrate_hbm.1, f32[8,256]{1,0:T(8,128)} %hcoef_hbm.1, bf16[256,1024]{1,0:T(8,128)(2,1)} %w_in_hbm.1, bf16[1024,256]{1,0:T(8,128)(2,1)} %w_out_hbm.1), custom_call_target="tpu_custom_call" | custom-call | tf_op jit(solution)/shard_map/pallas_call | solution.py:488
  37.6 1.4 %shard_map.74 = bf16[4096,256]{1,0:T(8,128)(2,1)} custom-call(bf16[4096,256]{1,0:T(8,128)(2,1)S(1)} %shard_map.73.src), custom_call_target="tpu_custom_call" | custom-call | tf_op jit(solution)/shard_map/pallas_call | solution.py:518

commit v5 on v4

--- a/solution.py
+++ b/solution.py
@@ -66,9 +66,10 @@
         def _():
             pl.semaphore_signal(barrier, inc=1, device_id=device, device_id_type=MESH)
 
-    def fetch_image(k):
-        part = pl.ds(pl.multiple_of(k * GROUP, GROUP), GROUP)
-        return pltpu.make_async_copy(image_hbm.at[:, part, :], img.at[:, part, :], img_sem.at[k])
+    def fetch_image(g):
+        part = pl.ds(pl.multiple_of(g % nk * GROUP, GROUP), GROUP)
+        lane = pl.ds(pl.multiple_of(g // nk * LANES, LANES), LANES)
+        return pltpu.make_async_copy(image_hbm.at[:, part, lane], img.at[:, part, lane], img_sem.at[g])
 
     fetches = [
         pltpu.make_async_copy(src, dst, arg_sem.at[i])
@@ -79,8 +80,8 @@
     ]
     for copy in fetches[:4]:
         copy.start()
-    for k in range(nk):
-        fetch_image(k).start()
+    for g in range(chunks):
+        fetch_image(g).start()
 
     for copy in fetches[:4]:
         copy.wait()
@@ -162,9 +163,7 @@
     def local(g):
         h, k = g // nk, g % nk
 
-        @pl.when(h == 0)
-        def _():
-            fetch_image(k).wait()
+        fetch_image(g).wait()
 
         @pl.when(g == nk)
         def _():
@@ -183,7 +182,7 @@
             return state
 
         zero = jnp.zeros((GROUP, LANES), jnp.float32)
-        state = lax.fori_loop(0, rows, step, (zero,) * modes, unroll=16)
+        state = lax.fori_loop(0, rows, step, (zero,) * modes, unroll=32)
         for m in range(modes):
             vtot[0, g, m] = state[m]
 
@@ -227,7 +226,7 @@
             out[at, :] = act.astype(jnp.float32)
             return carry
 
-        lax.fori_loop(0, rows, correct, 0, unroll=16)
+        lax.fori_loop(0, rows, correct, 0, unroll=32)
         p, q = spread(ptab, 1, h), spread(qtab, 1, h)
 
         def group(j, carry):
@@ -338,7 +337,7 @@
                 out[at, :] = out[at, :] + total([here[m:m + 1, :] * carried[m] for m in range(modes)])
                 return carry
 
-            lax.fori_loop(0, cols, correct, 0, unroll=16)
+            lax.fori_loop(0, cols, correct, 0, unroll=32)
 
     def mlp(i):
         line = jnp.concatenate(
@@ -510,7 +509,7 @@
             pltpu.SemaphoreType.DMA((strips * HOPS,)),
             pltpu.SemaphoreType.DMA((strips,)),
             pltpu.SemaphoreType.DMA((strips,)),
-            pltpu.SemaphoreType.DMA((cols // GROUP,)),
+            pltpu.SemaphoreType.DMA((chunks,)),
             pltpu.SemaphoreType.DMA((6,)),
         ],
         compiler_params=pltpu.CompilerParams(collective_id=0, has_side_effects=True, vmem_limit_bytes=67043328 - rows * cols * channels * 2 - 4096),

time: 39.2 us -> 38.9 us (level)
  no operation moved by 1% of the time
where the time goes in v5:
time: 38.9 us; the launch traced here: 38.7 us
  Pallas kernels  38.7 us (99%)
    pallas_call x1, Pallas kernels, on_device(): pl.pallas_call(functools.partial(layer_kernel, nrow, ncol, rows, cols, mo...  37.3 us
    pallas_call x1, Pallas kernels, on_device(): pl.pallas_call(emit, out_shape=jax.ShapeDtypeStruct((rows * cols, channel...  1.38 us

profile of v5, /device:TPU:28, one launch (start us, length us, event | category | flops | bytes accessed | tf_op | source)
XLA Modules:
  0.0 38.7 jit_solution(9019677910654878199)
XLA Ops:
  0.0 37.3 %shard_map.73.src = bf16[4096,256]{1,0:T(8,128)(2,1)S(1)} custom-call(bf16[64,64,256]{2,1,0:T(8,128)(2,1)} %image_hbm.1, f32[8,256]{1,0:T(8,128)} %vrate_hbm.1, f32[8,256]{1,0:T(8,128)} %vcoef_hbm.1, f32[8,256]{1,0:T(8,128)} %hrate_hbm.1, f32[8,256]{1,0:T(8,128)} %hcoef_hbm.1, bf16[256,1024]{1,0:T(8,128)(2,1)} %w_in_hbm.1, bf16[1024,256]{1,0:T(8,128)(2,1)} %w_out_hbm.1), custom_call_target="tpu_custom_call" | custom-call | tf_op jit(solution)/shard_map/pallas_call | solution.py:487
  37.3 1.4 %shard_map.74 = bf16[4096,256]{1,0:T(8,128)(2,1)} custom-call(bf16[4096,256]{1,0:T(8,128)(2,1)S(1)} %shard_map.73.src), custom_call_target="tpu_custom_call" | custom-call | tf_op jit(solution)/shard_map/pallas_call | solution.py:517
